TPU v7x, 32 devices: a whole 2x2x4 slice. The times are simulated.
32 devices in a mesh: pb: 4 (over y, core), ka: 8 (over z, x).
Axes of the slice: x: 2, y: 2, z: 4, core: 2. Of those that a mesh axis runs over, the one named last changes fastest.
Arguments:
- queries: float32 [2048, 128], P('pb'), may hold values from -36 to 36
- cache_keys: float32 [65536, 128], P('ka'), may hold values from -4 to 4
- cache_values: float32 [65536, 128], P('ka'), may hold values from -6 to 6
- kept_index: int32 [4096], P('ka'), may hold values from 0 to 65535, as said below
Outputs:
- fitted: float32 [4096, 128], P('ka')
Inputs may be any that keep to these rules, and one draw needn't show every extreme that they name: `kept_index`: Increasing; the t-th kept index lies among the cache rows t * (16) to (t + 1) * 16 - 1, so the kept keys of a device are rows of its own block of the cache.
All inputs are finite; a program needn't handle non-finite values.
Results may differ from a plain program's by a relative error of at most 0.0003.
Values sent between devices are 32-bit elements; how exact they have to be, the bound alone decides.
A program may use at most 128 MiB of HBM per device.

v0:
```python
import math

import jax
import jax.numpy as jnp
from jax import lax
from jax.sharding import PartitionSpec as P

ITERS = 2


ridge_weight = 0.01
highest = lax.Precision.HIGHEST


def merged_2(part, axis, combine):
    gathered = jax.tree.map(lambda a: lax.all_gather(a, axis), part)

    def take(source):
        return jax.tree.map(lambda a: lax.dynamic_index_in_dim(a, source, 0, False), gathered)

    return lax.fori_loop(
        1, lax.axis_size(axis), lambda source, state: combine(state, take(source)), take(0)
    )


def contract_rows(left_side, right_side):
    return lax.dot_general(
        left_side,
        right_side,
        (((0,), (0,)), ((), ())),
        precision=highest,
        preferred_element_type=jnp.float32,
    )


def contract_cols(left_side, right_side):
    return lax.dot_general(
        left_side,
        right_side,
        (((1,), (1,)), ((), ())),
        precision=highest,
        preferred_element_type=jnp.float32,
    )


def joint_scale(top_one, total_one, top_two, total_two):
    top_joint = jnp.maximum(top_one, top_two)
    factor_one = jnp.exp(top_one - top_joint)
    factor_two = jnp.exp(top_two - top_joint)
    return (top_joint, total_one * factor_one + total_two * factor_two, factor_one, factor_two)


def combine_target(part_one, part_two):
    top_joint, total_sum, factor_one, factor_two = joint_scale(
        part_one[0], part_one[1], part_two[0], part_two[1]
    )
    numerator = part_one[2] * factor_one[:, None] + part_two[2] * factor_two[:, None]
    return (top_joint, total_sum, numerator)


def combine_stats(part_one, part_two):
    target_part = combine_target(part_one[0:3], part_two[0:3])
    kept_top, kept_total, factor_one, factor_two = joint_scale(
        part_one[3], part_one[4], part_two[3], part_two[4]
    )
    return target_part + (kept_top, kept_total)


def key_rows(weights, updates):
    return lax.psum(contract_rows(weights, updates), "pb")


def forward_terms(weights, direction):
    return (
        jnp.dot(weights, direction, precision=highest, preferred_element_type=jnp.float32),
        jnp.sum(direction * direction, axis=0),
    )


def residual_total(column_part):
    return lax.psum(column_part, "ka")


def direction_total(column_part):
    return lax.psum(column_part, "ka")


def shards(queries, cache_keys, cache_values, kept_index):
    head_width = queries.shape[1]
    inverse_root = 1.0 / math.sqrt(head_width)
    cache_rows = cache_keys.shape[0]
    block_size = min(1024, cache_rows)
    target_stats = None
    for block_number in range(cache_rows // block_size):
        keys_block = lax.slice_in_dim(
            cache_keys, block_number * block_size, (block_number + 1) * block_size, axis=0
        )
        values_block = lax.slice_in_dim(
            cache_values, block_number * block_size, (block_number + 1) * block_size, axis=0
        )
        scores = contract_cols(queries, keys_block) * inverse_root
        top_block = jnp.max(scores, axis=1)
        exponent_block = jnp.exp(scores - top_block[:, None])
        stats_block = (
            top_block,
            jnp.sum(exponent_block, axis=1),
            jnp.dot(
                exponent_block, values_block, precision=highest, preferred_element_type=jnp.float32
            ),
        )
        target_stats = (
            stats_block if target_stats is None else combine_target(target_stats, stats_block)
        )
    local_kept = kept_index - lax.axis_index("ka") * cache_rows
    kept_keys = jnp.take(cache_keys, local_kept, axis=0)
    kept_scores = contract_cols(queries, kept_keys) * inverse_root
    kept_top = jnp.max(kept_scores, axis=1)
    kept_exponent = jnp.exp(kept_scores - kept_top[:, None])
    merged = merged_2(
        (
            target_stats[0],
            target_stats[1],
            target_stats[2],
            kept_top,
            jnp.sum(kept_exponent, axis=1),
        ),
        "ka",
        combine_stats,
    )
    target = merged[2] / merged[1][:, None]
    weights = kept_exponent * (jnp.exp(kept_top - merged[3]) / merged[4])[:, None]
    residual = key_rows(weights, target)
    fitted = jnp.zeros_like(residual)
    direction = residual
    norm_now = residual_total(jnp.sum(residual * residual, axis=0))
    for iteration in range(ITERS):
        final_turn = iteration + 1 == ITERS
        update_part, square_part = forward_terms(weights, direction)
        updates = lax.psum(update_part, "ka")
        operator_image = key_rows(weights, updates) + ridge_weight * direction
        step_length = norm_now / direction_total(jnp.sum(direction * operator_image, axis=0))
        fitted = fitted + step_length * direction
        if not final_turn:
            residual = residual - step_length * operator_image
            norm_next = residual_total(jnp.sum(residual * residual, axis=0))
            direction = residual + norm_next / norm_now * direction
            norm_now = norm_next
    return fitted


def solution(mesh):
    in_specs = (P("pb", None), P("ka", None), P("ka", None), P("ka"))
    out_specs = P("ka", None)
    return jax.shard_map(shards, mesh=mesh, in_specs=in_specs, out_specs=out_specs, check_vma=False)
```

profile of v0, /device:TPU:0, one launch (start us, length us, event | category | flops | bytes accessed | tf_op | source)
XLA Modules:
  0.0 488.6 jit_solution(1318856065512095628)
XLA Ops:
  6.5 0.9 copy-done
  7.5 3.1 multiply_reduce_fusion
  10.6 3.0 multiply_reduce_fusion.1
  13.7 2.0 multiply_reduce_fusion.2
  15.6 2.0 multiply_reduce_fusion.3
  17.6 2.0 multiply_reduce_fusion.4
  19.6 2.0 multiply_reduce_fusion.5
  21.6 2.1 multiply_reduce_fusion.6
  23.7 2.0 multiply_reduce_fusion.7
  25.8 2.0 fusion.18
  27.8 2.0 fusion.19
  29.8 2.0 fusion.20
  31.8 2.0 fusion.21
  33.9 2.2 fusion.22
  36.1 2.0 fusion.23
  38.1 2.1 fusion.36
  40.2 2.7 fusion.37
  43.0 0.5 fusion.16
  43.5 1.1 copy-done.2
  44.6 0.5 fusion.14
  45.1 0.1 copy-done.4
  45.2 0.5 fusion.12
  45.8 0.6 copy-done.6
  46.4 0.5 fusion.10
  46.9 0.1 copy-done.8
  47.0 0.5 fusion.8
  47.5 0.6 copy-done.10
  48.1 0.5 fusion.6
  48.7 0.5 fusion.4
  49.2 0.6 copy-done.14
  49.8 0.5 fusion.2
  50.4 28.0 %all-gather.3 = f32[8,1,512]{2,1,0:T(1,128)S(1)} all-gather(f32[1,1,512]{2,1,0:T(1,128)S(1)} %get-tuple-element.319), channel_id=1, replica_groups=mesh['pb'=4,'ka'=8] {'ka'}, dimensions={0}, use_global_device_ids=true | all-gather | bytes 18432 | tf_op jit(solution)/shard_map/all_gather | solution.py:16
  78.4 26.3 %all-gather.4 = f32[8,1,512]{2,1,0:T(1,128)S(1)} all-gather(f32[1,1,512]{2,1,0:T(1,128)S(1)} %get-tuple-element.318), channel_id=1, replica_groups=mesh['pb'=4,'ka'=8] {'ka'}, dimensions={0}, use_global_device_ids=true | all-gather | bytes 18432 | tf_op jit(solution)/shard_map/all_gather | solution.py:16
  104.8 3.2 gather_fusion
  108.0 1.1 fusion.106
  109.0 26.0 %all-gather.5 = f32[8,1,512]{2,1,0:T(1,128)S(1)} all-gather(f32[1,1,512]{2,1,0:T(1,128)S(1)} %bitcast.74), channel_id=3, replica_groups=mesh['pb'=4,'ka'=8] {'ka'}, dimensions={0}, use_global_device_ids=true | all-gather | bytes 18432 | tf_op jit(solution)/shard_map/all_gather | solution.py:16
  135.1 0.2 fusion.55
  135.3 26.0 %all-gather.6 = f32[8,1,512]{2,1,0:T(1,128)S(1)} all-gather(f32[1,1,512]{2,1,0:T(1,128)S(1)} %bitcast.91), channel_id=4, replica_groups=mesh['pb'=4,'ka'=8] {'ka'}, dimensions={0}, use_global_device_ids=true | all-gather | bytes 18432 | tf_op jit(solution)/shard_map/all_gather | solution.py:16
  161.3 1.0 slice.80
  162.2 9.3 %while.23 = (s32[]{:T(128)}, f32[512]{0:T(512)S(1)}, f32[512]{0:T(512)S(1)}, f32[512,128]{1,0:T(8,128)S(1)}, f32[512]{0:T(512)S(1)}, /*index=5*/f32[512]{0:T(512...) while((s32[]{:T(128)}, f32[512]{0:T(512)S(1)}, ...), condition=%wide.region_19.20_spmd, body=%wide.region_18.19_spmd.sunk | while | flops 202757 | bytes 835779 | solution.py:21
  162.3 1.2 fusion.120
  163.7 1.2 fusion.120
  165.0 1.2 fusion.120
  166.3 1.2 fusion.120
  167.6 1.2 fusion.120
  169.0 1.2 fusion.120
  170.3 1.2 fusion.120
  171.5 1.8 fusion.88
  173.4 29.4 %all-reduce.7.cloned.1.call-done = f32[512,128]{1,0:T(8,128)} async-done(((f32[512,128]{1,0:T(8,128)}), f32[512,128]{1,0:T(8,128)}) %all-reduce.7.cloned.1.call-update) | async-done | bytes 262160 | tf_op jit(solution)/shard_map/psum | solution.py:70
  202.8 3.5 fusion.86
  206.4 70.7 %all-reduce.9.cloned.1.call-done = f32[512,128]{1,0:T(8,128)} async-done(((f32[512,128]{1,0:T(8,128)}), f32[512,128]{1,0:T(8,128)}) %all-reduce.9.cloned.1.call-update) | async-done | bytes 262160 | tf_op jit(solution)/shard_map/psum | solution.py:139
  277.0 2.7 fusion.84
  279.8 31.4 %all-reduce.11.cloned.1.call-done = f32[512,128]{1,0:T(8,128)} async-done(((f32[512,128]{1,0:T(8,128)}), f32[512,128]{1,0:T(8,128)}) %all-reduce.11.cloned.1.call-update) | async-done | bytes 262160 | tf_op jit(solution)/shard_map/psum | solution.py:70
  311.2 1.0 multiply_reduce_fusion.10
  312.2 21.3 %all-reduce = (f32[128]{0:T(128)S(1)}, f32[128]{0:T(128)S(1)}) all-reduce(f32[128]{0:T(128)S(1)} %get-tuple-element.277, f32[128]{0:T(128)S(1)} %get-tuple-element.276), channel_id=1, replica_groups=mesh['pb'=4,'ka'=8] {'ka'}, use_global_device_ids=true, to_apply=%region_22.23 | all-reduce | flops 256 | bytes 2048 | tf_op jit(solution)/shard_map/psum | solution.py:81
  333.6 1.0 multiply_reduce_fusion.9
  334.6 17.3 %psum.68 = f32[128]{0:T(128)S(1)} all-reduce(f32[128]{0:T(128)S(1)} %multiply_reduce_fusion.9), channel_id=1, replica_groups=mesh['pb'=4,'ka'=8] {'ka'}, use_global_device_ids=true, to_apply=%region_28.29 | all-reduce | flops 128 | bytes 1024 | tf_op jit(solution)/shard_map/psum | solution.py:81
  351.9 3.5 fusion.82
  355.5 68.5 %all-reduce.13.cloned.1.call-done = f32[512,128]{1,0:T(8,128)} async-done(((f32[512,128]{1,0:T(8,128)}), f32[512,128]{1,0:T(8,128)}) %all-reduce.13.cloned.1.call-update) | async-done | bytes 262160 | tf_op jit(solution)/shard_map/psum | solution.py:139
  424.0 2.7 fusion.80
  426.7 31.4 %all-reduce.15.cloned.1.call-done = f32[512,128]{1,0:T(8,128)} async-done(((f32[512,128]{1,0:T(8,128)}), f32[512,128]{1,0:T(8,128)}) %all-reduce.15.cloned.1.call-update) | async-done | bytes 262160 | tf_op jit(solution)/shard_map/psum | solution.py:70
  458.1 1.1 multiply_reduce_fusion.8
  459.2 21.3 %psum.71 = f32[128]{0:T(128)S(1)} all-reduce(f32[128]{0:T(128)S(1)} %multiply_reduce_fusion.8), channel_id=1, replica_groups=mesh['pb'=4,'ka'=8] {'ka'}, use_global_device_ids=true, to_apply=%region_32.33 | all-reduce | flops 128 | bytes 1024 | tf_op jit(solution)/shard_map/psum | solution.py:85
  480.5 0.8 multiply_add_fusion.2
  (98 shorter events, 1.0 us)
Async XLA Ops:
  6.5 1.0 copy-start
  6.5 154.7 %all-gather.9.cloned.1.call-start = ((), (), s32[]{:S(2)}) async-start(), calls=%async_computation.5 | async-start | bytes 2359296 | tf_op jit(solution)/shard_map/all_gather | solution.py:16
  7.5 6.2 %copy-start.15 = (f32[8192,128]{1,0:T(8,128)S(1)}, f32[8192,128]{1,0:T(8,128)}, u32[]{:S(2)}) copy-start(f32[8192,128]{1,0:T(8,128)} %param.7) | copy-start | bytes 12582916
  13.6 12.1 %copy-start.1 = (f32[512,1024]{1,0:T(8,128)}, f32[512,1024]{1,0:T(8,128)S(1)}, u32[]{:S(2)}) copy-start(f32[512,1024]{1,0:T(8,128)S(1)} %get-tuple-element.346) | copy-start | bytes 6291460
  15.6 12.2 %copy-start.3 = (f32[512,1024]{1,0:T(8,128)}, f32[512,1024]{1,0:T(8,128)S(1)}, u32[]{:S(2)}) copy-start(f32[512,1024]{1,0:T(8,128)S(1)} %get-tuple-element.348) | copy-start | bytes 6291460
  17.6 12.2 %copy-start.5 = (f32[512,1024]{1,0:T(8,128)}, f32[512,1024]{1,0:T(8,128)S(1)}, u32[]{:S(2)}) copy-start(f32[512,1024]{1,0:T(8,128)S(1)} %get-tuple-element.350) | copy-start | bytes 6291460
  19.6 12.2 %copy-start.7 = (f32[512,1024]{1,0:T(8,128)}, f32[512,1024]{1,0:T(8,128)S(1)}, u32[]{:S(2)}) copy-start(f32[512,1024]{1,0:T(8,128)S(1)} %get-tuple-element.352) | copy-start | bytes 6291460
  21.6 12.3 %copy-start.9 = (f32[512,1024]{1,0:T(8,128)}, f32[512,1024]{1,0:T(8,128)S(1)}, u32[]{:S(2)}) copy-start(f32[512,1024]{1,0:T(8,128)S(1)} %get-tuple-element.354) | copy-start | bytes 6291460
  21.6 4.2 copy-start.18
  23.7 12.4 %copy-start.11 = (f32[512,1024]{1,0:T(8,128)}, f32[512,1024]{1,0:T(8,128)S(1)}, u32[]{:S(2)}) copy-start(f32[512,1024]{1,0:T(8,128)S(1)} %get-tuple-element.356) | copy-start | bytes 6291460
  25.7 12.4 %copy-start.13 = (f32[512,1024]{1,0:T(8,128)}, f32[512,1024]{1,0:T(8,128)S(1)}, u32[]{:S(2)}) copy-start(f32[512,1024]{1,0:T(8,128)S(1)} %get-tuple-element.358) | copy-start | bytes 6291460
  43.0 159.8 %all-reduce.7.cloned.1.call-start = ((), (), s32[]{:S(2)}) async-start(), calls=%async_computation | async-start | bytes 524288 | tf_op jit(solution)/shard_map/psum | solution.py:70
  43.0 1.6 copy-start.2
  43.0 2.2 copy-start.4
  44.6 1.7 copy-start.6
  45.2 1.7 copy-start.8
  46.4 1.7 copy-start.10
  47.0 1.7 copy-start.12
  48.1 1.7 copy-start.14
  48.7 56.0 %copy-start.19 = (s32[512]{0:T(512)S(1)}, s32[512]{0:T(512)}, u32[]{:S(2)}) copy-start(s32[512]{0:T(512)} %param.9) | copy-start | bytes 6148
  173.4 103.7 %all-reduce.9.cloned.1.call-start = ((), (), s32[]{:S(2)}) async-start(), calls=%async_computation.1 | async-start | bytes 524288 | tf_op jit(solution)/shard_map/psum | solution.py:139
  202.8 108.4 %copy-start.16 = (f32[512,128]{1,0:T(8,128)S(1)}, f32[512,128]{1,0:T(8,128)}, u32[]{:S(2)}) copy-start(f32[512,128]{1,0:T(8,128)} %all-reduce.7.cloned.1.call-done) | copy-start | bytes 786436
  206.3 104.8 %all-reduce.11.cloned.1.call-start = ((), (), s32[]{:S(2)}) async-start(), calls=%async_computation.2 | async-start | bytes 524288 | tf_op jit(solution)/shard_map/psum | solution.py:70
  279.8 144.2 %all-reduce.13.cloned.1.call-start = ((), (), s32[]{:S(2)}) async-start(), calls=%async_computation.3 | async-start | bytes 524288 | tf_op jit(solution)/shard_map/psum | solution.py:139
  334.6 123.5 %copy-start.17 = (f32[512,128]{1,0:T(8,128)S(1)}, f32[512,128]{1,0:T(8,128)}, u32[]{:S(2)}) copy-start(f32[512,128]{1,0:T(8,128)} %all-reduce.11.cloned.1.call-done) | copy-start | bytes 786436
  355.4 102.7 %all-reduce.15.cloned.1.call-start = ((), (), s32[]{:S(2)}) async-start(), calls=%async_computation.4 | async-start | bytes 524288 | tf_op jit(solution)/shard_map/psum | solution.py:70
Sparse Core Ops, SparseCore 0:
  43.1 52.1 all-gather.8
  173.5 29.2 all-reduce.6
  206.5 70.5 all-reduce.8
  279.9 31.2 all-reduce.10
  355.6 68.3 all-reduce.12
  426.8 31.2 all-reduce.14
where the time goes:
time: 498 us; the launch traced here: 489 us
  waiting for transfers between devices  231 us (46%)
  blocking collectives  166 us (33%)
  matrix products  50.5 us (10%)
  other arithmetic  17.1 us (3%)
  between operations  14.2 us (3%)
  local copies, waits for them, and re-layouts  8.61 us (2%)
    psum x2, waiting for transfers between devices, shards(): updates = lax.psum(update_part, 'ka')  139 us
    all_gather x4, blocking collectives, merged_2(): gathered = jax.tree.map(lambda a: lax.all_gather(a, axis), part)  106 us
    psum x3, waiting for transfers between devices, key_rows(): return lax.psum(contract_rows(weights, updates), 'pb')  92.1 us
    psum x2, blocking collectives, residual_total(): return lax.psum(column_part, 'ka')  38.6 us
    psum x1, blocking collectives, direction_total(): return lax.psum(column_part, 'ka')  21.3 us
    dot_general x9, matrix products, contract_cols(): lax.dot_general(left_side, right_side, (((1,), (1,)), ((), ())), precisio...  19.2 us
    dot_general x8, matrix products, shards(): jnp.dot(exponent_block, values_block, precision=highest, preferred_elemen...  17 us
  transfers between devices with their start and end apart: 6, of which 5 were waited for; matrix products, arithmetic and copies ran while one was open for 2% of the time, Pallas kernels for 0%

commit v1 on v0

v1 whole, which is shorter than its diff:
```python
import math

import jax
import jax.numpy as jnp
from jax import lax
from jax.sharding import PartitionSpec as P

ITERS = 2


ridge_weight = 0.01
highest = lax.Precision.HIGHEST


def contract(left_side, right_side, left_dim, right_dim):
    return lax.dot_general(
        left_side,
        right_side,
        (((left_dim,), (right_dim,)), ((), ())),
        precision=highest,
        preferred_element_type=jnp.float32,
    )


def column_sums(left_side, right_side):
    return jnp.sum(left_side * right_side, axis=0, keepdims=True)


def padded(rows, *tail):
    used = sum(part.shape[0] for part in tail)
    fill = jnp.zeros((-used % 8, rows.shape[1]), rows.dtype)
    return jnp.concatenate((rows,) + tail + (fill,), axis=0)


def shards(queries, cache_keys, cache_values, kept_index):
    query_rows, head_width = queries.shape
    inverse_root = 1.0 / math.sqrt(head_width)
    cache_rows = cache_keys.shape[0]
    block_size = min(1024, cache_rows)
    blocks = cache_rows // block_size

    local_kept = kept_index - lax.axis_index("ka") * cache_rows
    kept_keys = jnp.take(cache_keys, local_kept, axis=0)
    kept_scores = contract(queries, kept_keys, 1, 1) * inverse_root
    kept_top = jnp.max(kept_scores, axis=1)
    kept_exponent = jnp.exp(kept_scores - kept_top[:, None])
    kept_total = jnp.sum(kept_exponent, axis=1)

    def step(block_number, state):
        top, total, numerator = state
        start = block_number * block_size
        keys_block = lax.dynamic_slice_in_dim(cache_keys, start, block_size, axis=0)
        values_block = lax.dynamic_slice_in_dim(cache_values, start, block_size, axis=0)
        scores = contract(queries, keys_block, 1, 1) * inverse_root
        top_next = jnp.maximum(top, jnp.max(scores, axis=1))
        factor = jnp.exp(top - top_next)
        exponent = jnp.exp(scores - top_next[:, None])
        return (
            top_next,
            total * factor + jnp.sum(exponent, axis=1),
            numerator * factor[:, None] + contract(exponent, values_block, 1, 0),
        )

    top, total, numerator = lax.fori_loop(
        0,
        blocks,
        step,
        (
            jnp.full((query_rows,), -jnp.inf, jnp.float32),
            jnp.zeros((query_rows,), jnp.float32),
            jnp.zeros((query_rows, head_width), jnp.float32),
        ),
    )

    stats = jnp.concatenate((top, total, kept_top, kept_total)).reshape(-1, head_width)
    gathered = lax.all_gather(padded(numerator, stats), "ka")
    shares = gathered.shape[0]
    gathered_stats = gathered[:, query_rows : query_rows + stats.shape[0]]
    gathered_stats = gathered_stats.reshape(shares, 4, query_rows)
    factors = jnp.exp(gathered_stats[:, 0] - jnp.max(gathered_stats[:, 0], axis=0))
    target_total = jnp.sum(gathered_stats[:, 1] * factors, axis=0)
    target = jnp.sum(gathered[:, :query_rows] * factors[:, :, None], axis=0)
    target = target / target_total[:, None]
    kept_joint = jnp.max(gathered_stats[:, 2], axis=0)
    joint_total = jnp.sum(gathered_stats[:, 3] * jnp.exp(gathered_stats[:, 2] - kept_joint), axis=0)
    weights = kept_exponent * (jnp.exp(kept_top - kept_joint) / joint_total)[:, None]

    residual = lax.psum(contract(weights, target, 0, 0), "pb")
    kept_rows = residual.shape[0]
    fitted = jnp.zeros_like(residual)
    direction = residual
    updates = None
    norm_now = None
    length_now = None
    for iteration in range(ITERS):
        final_turn = iteration + 1 == ITERS
        forward = contract(weights, residual, 1, 0)
        if iteration == 0:
            summed = lax.psum(padded(forward, column_sums(residual, residual)), "ka")
            updates = summed[:query_rows]
            norm_now = summed[query_rows : query_rows + 1]
            length_now = norm_now
        else:
            summed = lax.psum(
                padded(
                    forward,
                    column_sums(residual, residual),
                    column_sums(residual, direction),
                ),
                "ka",
            )
            norm_next = summed[query_rows : query_rows + 1]
            crossed = summed[query_rows + 1 : query_rows + 2]
            ratio = norm_next / norm_now
            direction = residual + ratio * direction
            updates = summed[:query_rows] + ratio * updates
            length_now = norm_next + 2.0 * ratio * crossed + ratio * ratio * length_now
            norm_now = norm_next
        energy = column_sums(updates, updates)
        if final_turn:
            energy = lax.psum(energy, "pb")
            fitted = fitted + norm_now / (energy + ridge_weight * length_now) * direction
        else:
            summed = lax.psum(padded(contract(weights, updates, 0, 0), energy), "pb")
            operator_image = summed[:kept_rows] + ridge_weight * direction
            energy = summed[kept_rows : kept_rows + 1]
            step_length = norm_now / (energy + ridge_weight * length_now)
            fitted = fitted + step_length * direction
            residual = residual - step_length * operator_image
    return fitted


def solution(mesh):
    in_specs = (P("pb", None), P("ka", None), P("ka", None), P("ka"))
    out_specs = P("ka", None)
    return jax.shard_map(shards, mesh=mesh, in_specs=in_specs, out_specs=out_specs, check_vma=False)
```

time: 498 us -> 370 us (0.74); the launches traced: 489 us -> 369 us
  blocking collectives: 166 us -> 5.66 us
  waiting for transfers between devices: 231 us -> 256 us
  matrix products: 50.5 us -> 70.8 us
    all_gather x4 -> x0, blocking collectives: 106 us -> none  [merged_2(): gathered = jax.tree.map(lambda a: lax.all_gather(a, axis), part)]
    psum x3 -> x1, blocking collectives: 60 us -> 5.66 us  [shards(): energy = lax.psum(energy, 'pb')]
    all_gather x1, waiting for transfers between devices: 0.01 us -> 52.8 us  [shards(): gathered = lax.all_gather(padded(numerator, stats), 'ka')]
    psum x5 -> x4, waiting for transfers between devices: 231 us -> 203 us  [the longest x1 71.7 us: shards(): lax.psum(padded(forward, column_sums(residual, residual), column_sums(res...]
    dot_general x22 -> x21, matrix products: 50.5 us -> 70.8 us  [contract(): lax.dot_general(left_side, right_side, (((left_dim,), (right_dim,)), ((),...]
    add x15 -> x9, other arithmetic: 9.41 us -> 0.93 us  [the longest x1 0.8 us: shards(): fitted + norm_now / (energy + ridge_weight * length_now) * direction]
  transfers between devices with their start and end apart: 6 -> 5, of which waited for: 5 -> 5; matrix products, arithmetic and copies ran while one was open for 2% -> 0% of each run, Pallas kernels for 0% -> 0%
where the time goes in v1:
time: 370 us; the launch traced here: 369 us
  waiting for transfers between devices  256 us (69%)
  matrix products  70.8 us (19%)
  other arithmetic  16.1 us (4%)
  between operations  13.2 us (4%)
  local copies, waits for them, and re-layouts  6.21 us (2%)
  blocking collectives  5.66 us (2%)
    psum x1, waiting for transfers between devices, shards(): lax.psum(padded(forward, column_sums(residual, residual), column_sums(res...  71.7 us
    dot_general x21, matrix products, contract(): lax.dot_general(left_side, right_side, (((left_dim,), (right_dim,)), ((),...  70.8 us
    psum x1, waiting for transfers between devices, shards(): summed = lax.psum(padded(forward, column_sums(residual, residual)), 'ka')  70.6 us
    all_gather x1, waiting for transfers between devices, shards(): gathered = lax.all_gather(padded(numerator, stats), 'ka')  52.8 us
    psum x1, waiting for transfers between devices, shards(): residual = lax.psum(contract(weights, target, 0, 0), 'pb')  30.5 us
    psum x1, waiting for transfers between devices, shards(): summed = lax.psum(padded(contract(weights, updates, 0, 0), energy), 'pb')  30.5 us
  transfers between devices with their start and end apart: 5, of which 5 were waited for; matrix products, arithmetic and copies ran while one was open for 0% of the time, Pallas kernels for 0%

profile of v1, /device:TPU:0, one launch (start us, length us, event | category | flops | bytes accessed | tf_op | source)
XLA Modules:
  0.0 368.8 jit_solution(18405595993020933643)
XLA Ops:
  6.5 0.7 compare_and_fusion
  7.3 3.2 gather_fusion
  10.5 64.1 %while.18 = (s32[]{:T(128)}, f32[512]{0:T(512)S(1)}, f32[512]{0:T(512)S(1)}, f32[512,128]{1,0:T(8,128)S(1)}, f32[8192,128]{1,0:T(8,128)}, /*index=5*/f32[512,128...) while((s32[]{:T(128)}, f32[512]{0:T(512)S(1)}, ...), condition=%wide.region_4.5_spmd.clone, body=%wide.region_1.0_spmd.clone.sunk | while | flops 1614481920 | bytes 8159415 | solution.py:64
  10.5 2.9 multiply_reduce_fusion.6
  13.5 0.4 fusion.60
  13.9 4.6 %fusion.62 = f32[512,128]{1,0:T(8,128)S(1)} fusion(f32[1024,512]{1,0:T(8,128)S(1)} %get-tuple-element.239, f32[512]{0:T(512)S(1)} %select_maximum_fusion.2, f32[8192,128]{1,0:T(8,128)} %get-tuple-element.270, s32[]{:T(128)S(6)} %select_n.27, f32[512,128]{1,0:T(8,128)S(1)} %get-tuple-element.256, f32[512]{0:T(512)S(1)} %get-tuple-element.241, ...), kind=kOutput, calls=%fused_computation.5.clone.1 | convolution fusion | flops 806551552 | bytes 3149829 | tf_op jit(solution)/shard_map/while/body/eval_jaxpr/dot_general | solution.py:16
  18.6 2.9 multiply_reduce_fusion.6
  21.5 0.4 fusion.60
  21.9 4.6 %fusion.62 = f32[512,128]{1,0:T(8,128)S(1)} fusion(f32[1024,512]{1,0:T(8,128)S(1)} %get-tuple-element.239, f32[512]{0:T(512)S(1)} %select_maximum_fusion.2, f32[8192,128]{1,0:T(8,128)} %get-tuple-element.270, s32[]{:T(128)S(6)} %select_n.27, f32[512,128]{1,0:T(8,128)S(1)} %get-tuple-element.256, f32[512]{0:T(512)S(1)} %get-tuple-element.241, ...), kind=kOutput, calls=%fused_computation.5.clone.1 | convolution fusion | flops 806551552 | bytes 3149829 | tf_op jit(solution)/shard_map/while/body/eval_jaxpr/dot_general | solution.py:16
  26.6 2.9 multiply_reduce_fusion.6
  29.5 0.4 fusion.60
  29.9 4.6 %fusion.62 = f32[512,128]{1,0:T(8,128)S(1)} fusion(f32[1024,512]{1,0:T(8,128)S(1)} %get-tuple-element.239, f32[512]{0:T(512)S(1)} %select_maximum_fusion.2, f32[8192,128]{1,0:T(8,128)} %get-tuple-element.270, s32[]{:T(128)S(6)} %select_n.27, f32[512,128]{1,0:T(8,128)S(1)} %get-tuple-element.256, f32[512]{0:T(512)S(1)} %get-tuple-element.241, ...), kind=kOutput, calls=%fused_computation.5.clone.1 | convolution fusion | flops 806551552 | bytes 3149829 | tf_op jit(solution)/shard_map/while/body/eval_jaxpr/dot_general | solution.py:16
  34.6 2.9 multiply_reduce_fusion.6
  37.5 0.4 fusion.60
  37.9 4.6 %fusion.62 = f32[512,128]{1,0:T(8,128)S(1)} fusion(f32[1024,512]{1,0:T(8,128)S(1)} %get-tuple-element.239, f32[512]{0:T(512)S(1)} %select_maximum_fusion.2, f32[8192,128]{1,0:T(8,128)} %get-tuple-element.270, s32[]{:T(128)S(6)} %select_n.27, f32[512,128]{1,0:T(8,128)S(1)} %get-tuple-element.256, f32[512]{0:T(512)S(1)} %get-tuple-element.241, ...), kind=kOutput, calls=%fused_computation.5.clone.1 | convolution fusion | flops 806551552 | bytes 3149829 | tf_op jit(solution)/shard_map/while/body/eval_jaxpr/dot_general | solution.py:16
  42.6 2.9 multiply_reduce_fusion.6
  45.5 0.4 fusion.60
  46.0 4.6 %fusion.62 = f32[512,128]{1,0:T(8,128)S(1)} fusion(f32[1024,512]{1,0:T(8,128)S(1)} %get-tuple-element.239, f32[512]{0:T(512)S(1)} %select_maximum_fusion.2, f32[8192,128]{1,0:T(8,128)} %get-tuple-element.270, s32[]{:T(128)S(6)} %select_n.27, f32[512,128]{1,0:T(8,128)S(1)} %get-tuple-element.256, f32[512]{0:T(512)S(1)} %get-tuple-element.241, ...), kind=kOutput, calls=%fused_computation.5.clone.1 | convolution fusion | flops 806551552 | bytes 3149829 | tf_op jit(solution)/shard_map/while/body/eval_jaxpr/dot_general | solution.py:16
  50.6 2.9 multiply_reduce_fusion.6
  53.6 0.4 fusion.60
  54.0 4.6 %fusion.62 = f32[512,128]{1,0:T(8,128)S(1)} fusion(f32[1024,512]{1,0:T(8,128)S(1)} %get-tuple-element.239, f32[512]{0:T(512)S(1)} %select_maximum_fusion.2, f32[8192,128]{1,0:T(8,128)} %get-tuple-element.270, s32[]{:T(128)S(6)} %select_n.27, f32[512,128]{1,0:T(8,128)S(1)} %get-tuple-element.256, f32[512]{0:T(512)S(1)} %get-tuple-element.241, ...), kind=kOutput, calls=%fused_computation.5.clone.1 | convolution fusion | flops 806551552 | bytes 3149829 | tf_op jit(solution)/shard_map/while/body/eval_jaxpr/dot_general | solution.py:16
  58.6 2.9 multiply_reduce_fusion.6
  61.6 0.4 fusion.60
  62.0 4.6 %fusion.62 = f32[512,128]{1,0:T(8,128)S(1)} fusion(f32[1024,512]{1,0:T(8,128)S(1)} %get-tuple-element.239, f32[512]{0:T(512)S(1)} %select_maximum_fusion.2, f32[8192,128]{1,0:T(8,128)} %get-tuple-element.270, s32[]{:T(128)S(6)} %select_n.27, f32[512,128]{1,0:T(8,128)S(1)} %get-tuple-element.256, f32[512]{0:T(512)S(1)} %get-tuple-element.241, ...), kind=kOutput, calls=%fused_computation.5.clone.1 | convolution fusion | flops 806551552 | bytes 3149829 | tf_op jit(solution)/shard_map/while/body/eval_jaxpr/dot_general | solution.py:16
  66.7 2.9 multiply_reduce_fusion.6
  69.6 0.4 fusion.60
  70.0 4.6 %fusion.62 = f32[512,128]{1,0:T(8,128)S(1)} fusion(f32[1024,512]{1,0:T(8,128)S(1)} %get-tuple-element.239, f32[512]{0:T(512)S(1)} %select_maximum_fusion.2, f32[8192,128]{1,0:T(8,128)} %get-tuple-element.270, s32[]{:T(128)S(6)} %select_n.27, f32[512,128]{1,0:T(8,128)S(1)} %get-tuple-element.256, f32[512]{0:T(512)S(1)} %get-tuple-element.241, ...), kind=kOutput, calls=%fused_computation.5.clone.1 | convolution fusion | flops 806551552 | bytes 3149829 | tf_op jit(solution)/shard_map/while/body/eval_jaxpr/dot_general | solution.py:16
  74.7 1.1 fusion.49
  75.7 0.2 fusion.14
  75.9 1.9 concatenate.27
  77.8 0.0 all-gather.3.cloned.1.call-update
  77.9 0.0 all-reduce.5.cloned.1.call-start
  77.9 52.8 %all-gather.3.cloned.1.call-done = f32[4224,128]{1,0:T(8,128)} async-done(((f32[528,128]{1,0:T(8,128)}), f32[4224,128]{1,0:T(8,128)}) %all-gather.3.cloned.1.call-update) | async-done | bytes 2162704 | tf_op jit(solution)/shard_map/all_gather | solution.py:76
  130.7 0.8 slice.56
  131.6 0.1 slice_reduce_fusion
  131.7 1.9 fusion.12
  133.6 1.8 fusion.21
  135.4 0.0 all-reduce.5.cloned.1.call-update
  135.5 0.0 all-reduce.7.cloned.1.call-start
  135.5 0.1 pad.9.clone
  135.6 30.5 %all-reduce.5.cloned.1.call-done = f32[512,128]{1,0:T(8,128)} async-done(((f32[512,128]{1,0:T(8,128)}), f32[512,128]{1,0:T(8,128)}) %all-reduce.5.cloned.1.call-update) | async-done | bytes 262160 | tf_op jit(solution)/shard_map/psum | solution.py:88
  166.1 1.0 multiply_reduce_fusion.4
  167.1 2.8 fusion.19
  169.9 0.8 maximum_maximum_fusion
  170.8 0.0 all-reduce.9.cloned.1.call-start
  170.8 70.6 %all-reduce.7.cloned.1.call-done = f32[520,128]{1,0:T(8,128)} async-done(((f32[520,128]{1,0:T(8,128)}), f32[520,128]{1,0:T(8,128)}) %all-reduce.7.cloned.1.call-update) | async-done | bytes 266256 | tf_op jit(solution)/shard_map/psum | solution.py:99
  241.5 1.1 multiply_reduce_fusion.3
  242.6 2.0 fusion.17
  244.6 0.8 maximum_maximum_fusion.1
  245.4 0.0 all-reduce.9.cloned.1.call-update
  245.4 0.2 all-reduce.11.cloned.1.call-start
  245.6 0.1 pad.3.clone
  245.7 30.5 %all-reduce.9.cloned.1.call-done = f32[520,128]{1,0:T(8,128)} async-done(((f32[520,128]{1,0:T(8,128)}), f32[520,128]{1,0:T(8,128)}) %all-reduce.9.cloned.1.call-update) | async-done | bytes 266256 | tf_op jit(solution)/shard_map/psum | solution.py:124
  276.2 0.8 fusion.44
  276.9 2.8 fusion.15
  279.7 1.0 multiply_reduce_fusion.2
  280.8 0.8 maximum_maximum_fusion.2
  281.6 0.0 all-reduce.11.cloned.1.call-update
  281.6 71.7 %all-reduce.11.cloned.1.call-done = f32[520,128]{1,0:T(8,128)} async-done(((f32[520,128]{1,0:T(8,128)}), f32[520,128]{1,0:T(8,128)}) %all-reduce.11.cloned.1.call-update) | async-done | bytes 266256 | tf_op jit(solution)/shard_map/psum | solution.py:104
  353.3 0.7 slice_divide_fusion
  354.0 1.0 fusion.24
  355.0 5.7 %psum.39 = f32[1,128]{1,0:T(1,128)S(1)} all-reduce(f32[1,128]{1,0:T(1,128)S(1)} %bitcast.57), channel_id=1, replica_groups=mesh['pb'=4,'ka'=8] {'pb'}, use_global_device_ids=true, to_apply=%region_20.21 | all-reduce | flops 128 | bytes 1024 | tf_op jit(solution)/shard_map/psum | solution.py:121
  360.7 0.8 fusion.45
  361.4 0.8 multiply_add_fusion
  (43 shorter events, 0.3 us)
Async XLA Ops:
  6.5 4.0 %copy-start = (f32[512,128]{1,0:T(8,128)S(1)}, f32[512,128]{1,0:T(8,128)}, u32[]{:S(2)}) copy-start(f32[512,128]{1,0:T(8,128)} %param.6) | copy-start | bytes 786436
  6.5 124.1 %all-gather.3.cloned.1.call-start = ((), (), s32[]{:S(2)}) async-start(), calls=%async_computation.4 | async-start | bytes 2433024 | tf_op jit(solution)/shard_map/all_gather | solution.py:76
  77.9 88.2 %all-reduce.5.cloned.1.call-start = ((), (), s32[]{:S(2)}) async-start(), calls=%async_computation | async-start | bytes 524288 | tf_op jit(solution)/shard_map/psum | solution.py:88
  135.5 106.0 %all-reduce.7.cloned.1.call-start = ((), (), s32[]{:S(2)}) async-start(), calls=%async_computation.1 | async-start | bytes 532480 | tf_op jit(solution)/shard_map/psum | solution.py:99
  169.9 107.0 %copy-start.1 = (f32[512,128]{1,0:T(8,128)S(1)}, f32[512,128]{1,0:T(8,128)}, u32[]{:S(2)}) copy-start(f32[512,128]{1,0:T(8,128)} %all-reduce.5.cloned.1.call-done) | copy-start | bytes 786436
  170.8 105.4 %all-reduce.9.cloned.1.call-start = ((), (), s32[]{:S(2)}) async-start(), calls=%async_computation.2 | async-start | bytes 532480 | tf_op jit(solution)/shard_map/psum | solution.py:124
  241.5 34.7 %copy-start.2 = (f32[520,128]{1,0:T(8,128)S(1)}, f32[520,128]{1,0:T(8,128)}, u32[]{:S(2)}) copy-start(f32[520,128]{1,0:T(8,128)} %all-reduce.7.cloned.1.call-done) | copy-start | bytes 798724
  245.4 107.9 %all-reduce.11.cloned.1.call-start = ((), (), s32[]{:S(2)}) async-start(), calls=%async_computation.3 | async-start | bytes 532480 | tf_op jit(solution)/shard_map/psum | solution.py:104
  276.2 85.3 %copy-start.3 = (f32[520,128]{1,0:T(8,128)S(1)}, f32[520,128]{1,0:T(8,128)}, u32[]{:S(2)}) copy-start(f32[520,128]{1,0:T(8,128)} %all-reduce.9.cloned.1.call-done) | copy-start | bytes 798724
Sparse Core Ops, SparseCore 0:
  78.0 52.6 all-gather.2
  135.6 30.4 all-reduce.4
  170.9 70.5 all-reduce.6
  245.5 30.6 all-reduce.8
  281.7 71.5 all-reduce.10

commit v2 on v1

v2 whole, which is shorter than its diff:
```python
import functools
import math

import jax
import jax.numpy as jnp
from jax import lax
from jax.experimental import pallas as pl
from jax.experimental.pallas import tpu as pltpu
from jax.sharding import PartitionSpec as P

ITERS = 2


ridge_weight = 0.01
highest = lax.Precision.HIGHEST


def contract(left_side, right_side, left_dim, right_dim):
    return lax.dot_general(
        left_side,
        right_side,
        (((left_dim,), (right_dim,)), ((), ())),
        precision=highest,
        preferred_element_type=jnp.float32,
    )


def column_sums(left_side, right_side):
    return jnp.sum(left_side * right_side, axis=0, keepdims=True)


def fit_kernel(
    ka_size,
    pb_size,
    part_ref,
    kept_ref,
    fitted_ref,
    flipped,
    stats_in,
    stats_all,
    ka_out,
    ka_in,
    ka_all,
    pb_out,
    pb_in,
    pb_all,
    tail_out,
    tail_in,
    ka_send,
    ka_recv,
    pb_send,
    pb_recv,
):
    ka_me = lax.axis_index("ka")
    pb_me = lax.axis_index("pb")
    width = fitted_ref.shape[1]
    query_rows = kept_ref.shape[0]
    kept_rows = kept_ref.shape[1]
    ka_share = query_rows // ka_size
    pb_share = kept_rows // pb_size

    def peer_of(axis, offset):
        size = ka_size if axis == "ka" else pb_size
        me = ka_me if axis == "ka" else pb_me
        return lax.rem(me + offset, size)

    barrier = pltpu.get_barrier_semaphore()
    for axis, size in (("ka", ka_size), ("pb", pb_size)):
        for offset in range(1, size):
            pl.semaphore_signal(
                barrier,
                inc=1,
                device_id={axis: peer_of(axis, offset)},
                device_id_type=pl.DeviceIdType.MESH,
            )
    pl.semaphore_wait(barrier, ka_size + pb_size - 2)

    def begin(axis, phase, source_of, target):
        size, send, recv = (
            (ka_size, ka_send, ka_recv) if axis == "ka" else (pb_size, pb_send, pb_recv)
        )
        copies = []
        for offset in range(1, size):
            peer = peer_of(axis, offset)
            copy = pltpu.make_async_remote_copy(
                src_ref=source_of(peer),
                dst_ref=target,
                send_sem=send.at[phase, offset],
                recv_sem=recv.at[phase, offset],
                device_id={axis: peer},
                device_id_type=pl.DeviceIdType.MESH,
            )
            copy.start()
            copies.append(copy)
        return copies

    def finish(copies):
        for copy in copies:
            copy.wait()

    def scattered_sum(axis, phase, value, tail, out, arrived, whole):
        me, size, share = (
            (ka_me, ka_size, ka_share) if axis == "ka" else (pb_me, pb_size, pb_share)
        )
        out[:, :share, :] = value.reshape(size, share, width)
        out[:, share:, :] = jnp.broadcast_to(tail[None], (size, 8, width))
        copies = begin(axis, phase, lambda peer: out.at[peer], arrived.at[me])
        arrived[me] = out[me]
        finish(copies)
        total = arrived[0]
        for source in range(1, size):
            total = total + arrived[source]
        whole[me] = total[:share]
        finish(begin(axis, phase + 1, lambda peer: whole.at[me], whole.at[me]))
        return whole[...].reshape(size * share, width), total[share:]

    def matmul(left_side, right_side):
        return jnp.dot(
            left_side, right_side, precision=highest, preferred_element_type=jnp.float32
        )

    def tail_rows(*rows):
        place = lax.broadcasted_iota(jnp.int32, (8, width), 0)
        tail = jnp.zeros((8, width), jnp.float32)
        for number, row in enumerate(rows):
            tail = jnp.where(place == number, row, tail)
        return tail

    copies = begin("ka", 0, lambda peer: part_ref.at[peer], stats_in.at[ka_me])
    stats_in[ka_me] = part_ref[ka_me]
    flipped[...] = kept_ref[...].T
    finish(copies)

    def column(source, number):
        return stats_in[source, :, width + number : width + number + 1]

    top = column(0, 0)
    kept_top = column(0, 2)
    for source in range(1, ka_size):
        top = jnp.maximum(top, column(source, 0))
        kept_top = jnp.maximum(kept_top, column(source, 2))
    total = jnp.zeros_like(top)
    kept_total = jnp.zeros_like(top)
    numerator = jnp.zeros((ka_share, width), jnp.float32)
    for source in range(ka_size):
        factor = jnp.exp(column(source, 0) - top)
        total = total + column(source, 1) * factor
        numerator = numerator + stats_in[source, :, :width] * factor
        kept_total = kept_total + column(source, 3) * jnp.exp(column(source, 2) - kept_top)
    lane = lax.broadcasted_iota(jnp.int32, (ka_share, width), 1)
    stats_all[ka_me, :, :width] = numerator / total
    stats_all[ka_me, :, width:] = jnp.where(lane == 0, kept_top, kept_total)
    finish(begin("ka", 1, lambda peer: stats_all.at[ka_me], stats_all.at[ka_me]))
    target = stats_all[:, :, :width].reshape(query_rows, width)
    joint_top = stats_all[:, :, width : width + 1].reshape(query_rows, 1)
    joint_total = stats_all[:, :, width + 1 : width + 2].reshape(query_rows, 1)
    own_top = part_ref[:, :, width + 2 : width + 3].reshape(query_rows, 1)
    scale = jnp.exp(own_top - joint_top) / joint_total

    no_tail = jnp.zeros((8, width), jnp.float32)
    residual, _ = scattered_sum(
        "pb",
        0,
        matmul(flipped[...], scale * target),
        no_tail,
        pb_out.at[0],
        pb_in.at[0],
        pb_all.at[0],
    )
    fitted = jnp.zeros_like(residual)
    direction = residual
    updates = None
    norm_now = None
    length_now = None
    for iteration in range(ITERS):
        forward = scale * matmul(kept_ref[...], residual)
        tail = tail_rows(column_sums(residual, residual), column_sums(residual, direction))
        summed, tail = scattered_sum(
            "ka",
            2 + 2 * iteration,
            forward,
            tail,
            ka_out.at[iteration],
            ka_in.at[iteration],
            ka_all.at[iteration],
        )
        norm_next = tail[0:1]
        if iteration == 0:
            updates = summed
            length_now = norm_next
        else:
            ratio = norm_next / norm_now
            direction = residual + ratio * direction
            updates = summed + ratio * updates
            length_now = norm_next + 2.0 * ratio * tail[1:2] + ratio * ratio * length_now
        norm_now = norm_next
        energy = tail_rows(column_sums(updates, updates))
        if iteration + 1 == ITERS:
            tail_out[...] = energy
            copies = begin("pb", 2 * ITERS, lambda peer: tail_out, tail_in.at[pb_me])
            tail_in[pb_me] = energy
            finish(copies)
            energy = tail_in[0]
            for source in range(1, pb_size):
                energy = energy + tail_in[source]
            step_length = norm_now / (energy[0:1] + ridge_weight * length_now)
            fitted_ref[...] = fitted + step_length * direction
        else:
            image, energy = scattered_sum(
                "pb",
                2 + 2 * iteration,
                matmul(flipped[...], scale * updates),
                energy,
                pb_out.at[iteration + 1],
                pb_in.at[iteration + 1],
                pb_all.at[iteration + 1],
            )
            step_length = norm_now / (energy[0:1] + ridge_weight * length_now)
            fitted = fitted + step_length * direction
            residual = residual - step_length * (image + ridge_weight * direction)


def fit(part, kept_exponent):
    ka_size, pb_size = lax.axis_size("ka"), lax.axis_size("pb")
    query_rows, kept_rows = kept_exponent.shape
    width = part.shape[1] // 2
    ka_share, pb_share = query_rows // ka_size, kept_rows // pb_size
    space = functools.partial(pltpu.VMEM, dtype=jnp.float32)
    return pl.pallas_call(
        functools.partial(fit_kernel, ka_size, pb_size),
        out_shape=jax.ShapeDtypeStruct((kept_rows, width), jnp.float32),
        in_specs=[pl.BlockSpec(memory_space=pltpu.VMEM)] * 2,
        out_specs=pl.BlockSpec(memory_space=pltpu.VMEM),
        scratch_shapes=[
            space((kept_rows, query_rows)),
            space((ka_size, ka_share, 2 * width)),
            space((ka_size, ka_share, 2 * width)),
            space((ITERS, ka_size, ka_share + 8, width)),
            space((ITERS, ka_size, ka_share + 8, width)),
            space((ITERS, ka_size, ka_share, width)),
            space((ITERS, pb_size, pb_share + 8, width)),
            space((ITERS, pb_size, pb_share + 8, width)),
            space((ITERS, pb_size, pb_share, width)),
            space((8, width)),
            space((pb_size, 8, width)),
            pltpu.SemaphoreType.DMA((2 + 2 * ITERS, ka_size)),
            pltpu.SemaphoreType.DMA((2 + 2 * ITERS, ka_size)),
            pltpu.SemaphoreType.DMA((2 * ITERS + 1, pb_size)),
            pltpu.SemaphoreType.DMA((2 * ITERS + 1, pb_size)),
        ],
        compiler_params=pltpu.CompilerParams(
            collective_id=0, has_side_effects=True, vmem_limit_bytes=40 * 1024 * 1024
        ),
    )(part.reshape(ka_size, ka_share, 2 * width), kept_exponent)


def shards(queries, cache_keys, cache_values, kept_index):
    query_rows, head_width = queries.shape
    inverse_root = 1.0 / math.sqrt(head_width)
    cache_rows = cache_keys.shape[0]
    block_size = min(1024, cache_rows)
    blocks = cache_rows // block_size

    local_kept = kept_index - lax.axis_index("ka") * cache_rows
    kept_keys = jnp.take(cache_keys, local_kept, axis=0)
    kept_scores = contract(queries, kept_keys, 1, 1) * inverse_root
    kept_top = jnp.max(kept_scores, axis=1)
    kept_exponent = jnp.exp(kept_scores - kept_top[:, None])
    kept_total = jnp.sum(kept_exponent, axis=1)

    def step(block_number, state):
        top, total, numerator = state
        start = block_number * block_size
        keys_block = lax.dynamic_slice_in_dim(cache_keys, start, block_size, axis=0)
        values_block = lax.dynamic_slice_in_dim(cache_values, start, block_size, axis=0)
        scores = contract(queries, keys_block, 1, 1) * inverse_root
        top_next = jnp.maximum(top, jnp.max(scores, axis=1))
        factor = jnp.exp(top - top_next)
        exponent = jnp.exp(scores - top_next[:, None])
        return (
            top_next,
            total * factor + jnp.sum(exponent, axis=1),
            numerator * factor[:, None] + contract(exponent, values_block, 1, 0),
        )

    top, total, numerator = lax.fori_loop(
        0,
        blocks,
        step,
        (
            jnp.full((query_rows,), -jnp.inf, jnp.float32),
            jnp.zeros((query_rows,), jnp.float32),
            jnp.zeros((query_rows, head_width), jnp.float32),
        ),
    )

    stats = jnp.stack((top, total, kept_top, kept_total), axis=1)
    stats = jnp.pad(stats, ((0, 0), (0, head_width - 4)))
    return fit(jnp.concatenate((numerator, stats), axis=1), kept_exponent)


def solution(mesh):
    in_specs = (P("pb", None), P("ka", None), P("ka", None), P("ka"))
    out_specs = P("ka", None)
    return jax.shard_map(shards, mesh=mesh, in_specs=in_specs, out_specs=out_specs, check_vma=False)
```

time: 370 us -> 161 us (0.44)
  waiting for transfers between devices: 256 us -> 0 us
  Pallas kernels: 0 us -> 89.5 us
  between operations: 13.2 us -> 0.08 us
  other arithmetic: 16.1 us -> 4.49 us
  matrix products: 70.8 us -> 61.5 us
  blocking collectives: 5.66 us -> 0 us
    psum x4 -> x0, waiting for transfers between devices: 203 us -> none  [the longest x1 71.7 us: shards(): lax.psum(padded(forward, column_sums(residual, residual), column_sums(res...]
    pallas_call x0 -> x1, Pallas kernels: none -> 89.5 us  [fit(): pl.pallas_call(functools.partial(fit_kernel, ka_size, pb_size), out_shape...]
    all_gather x1 -> x0, waiting for transfers between devices: 52.8 us -> none  [shards(): gathered = lax.all_gather(padded(numerator, stats), 'ka')]
    dot_general x21 -> x17, matrix products: 70.8 us -> 61.5 us  [contract(): lax.dot_general(left_side, right_side, (((left_dim,), (right_dim,)), ((),...]
    reduce_sum x7 -> x0, other arithmetic: 6.39 us -> none  [the longest x4 4.21 us: column_sums(): return jnp.sum(left_side * right_side, axis=0, keepdims=True)]
    psum x1 -> x0, blocking collectives: 5.66 us -> none  [shards(): energy = lax.psum(energy, 'pb')]
  transfers between devices with their start and end apart: 5 -> 0, of which waited for: 5 -> 0; matrix products, arithmetic and copies ran while one was open for 0% -> 0% of each run, Pallas kernels for 0% -> 0%
where the time goes in v2:
time: 161 us; the launch traced here: 160 us
  Pallas kernels  89.5 us (56%)
  matrix products  61.5 us (38%)
  other arithmetic  4.49 us (3%)
  local copies, waits for them, and re-layouts  4.27 us (3%)
    pallas_call x1, Pallas kernels, fit(): pl.pallas_call(functools.partial(fit_kernel, ka_size, pb_size), out_shape...  89.5 us
    dot_general x17, matrix products, contract(): lax.dot_general(left_side, right_side, (((left_dim,), (right_dim,)), ((),...  61.5 us
    gather x1, local copies, waits for them, and re-layouts, shards(): kept_keys = jnp.take(cache_keys, local_kept, axis=0)  3.22 us

profile of v2, /device:TPU:0, one launch (start us, length us, event | category | flops | bytes accessed | tf_op | source)
XLA Modules:
  0.0 160.4 jit_solution(14942061639047467152)
XLA Ops:
  0.0 0.0 copy-start
  0.0 0.7 compare_and_fusion
  0.7 3.2 %gather_fusion = f32[512,128]{1,0:T(8,128)S(1)} fusion(f32[8192,128]{1,0:T(8,128)} %param.7, s32[1024]{0:T(1024)S(1)} %pad_clamp_fusion), kind=kCustom, calls=%fused_computation | custom fusion | bytes 526336 | tf_op jit(solution)/shard_map/jit(_take)/gather | solution.py:265
  4.0 0.0 copy-done
  4.0 64.3 %while.18 = (s32[]{:T(128)}, f32[512]{0:T(512)S(1)}, f32[512]{0:T(512)S(1)}, f32[512,128]{1,0:T(8,128)S(1)}, f32[8192,128]{1,0:T(8,128)}, /*index=5*/f32[512,128...) while((s32[]{:T(128)}, f32[512]{0:T(512)S(1)}, ...), condition=%wide.region_3.4_spmd.clone, body=%wide.region_0.3_spmd.clone.sunk | while | flops 1614481920 | bytes 8159415 | solution.py:286
  4.0 2.9 %multiply_reduce_fusion.2 = (f32[512]{0:T(512)S(1)}, f32[1024,512]{1,0:T(8,128)S(1)}) fusion(f32[512,128]{1,0:T(8,128)S(1)} %get-tuple-element.260, f32[8192,128]{1,0:T(8,128)} %get-tuple-element.259, s32[]{:T(128)S(6)} %select_n.27), kind=kOutput, calls=%fused_computation.2.clone.1 | convolution fusion | flops 806354432 | bytes 2885636 | tf_op jit(solution)/shard_map/while/body/eval_jaxpr/dot_general | solution.py:19
  6.9 0.4 fusion.28
  7.4 4.6 %fusion.30 = f32[512,128]{1,0:T(8,128)S(1)} fusion(f32[1024,512]{1,0:T(8,128)S(1)} %get-tuple-element.230, f32[512]{0:T(512)S(1)} %select_maximum_fusion.5, f32[8192,128]{1,0:T(8,128)} %get-tuple-element.261, s32[]{:T(128)S(6)} %select_n.27, f32[512,128]{1,0:T(8,128)S(1)} %get-tuple-element.247, f32[512]{0:T(512)S(1)} %get-tuple-element.232, ...), kind=kOutput, calls=%fused_computation.5.clone.1 | convolution fusion | flops 806551552 | bytes 3149829 | tf_op jit(solution)/shard_map/while/body/eval_jaxpr/dot_general | solution.py:19
  12.0 2.9 %multiply_reduce_fusion.2 = (f32[512]{0:T(512)S(1)}, f32[1024,512]{1,0:T(8,128)S(1)}) fusion(f32[512,128]{1,0:T(8,128)S(1)} %get-tuple-element.260, f32[8192,128]{1,0:T(8,128)} %get-tuple-element.259, s32[]{:T(128)S(6)} %select_n.27), kind=kOutput, calls=%fused_computation.2.clone.1 | convolution fusion | flops 806354432 | bytes 2885636 | tf_op jit(solution)/shard_map/while/body/eval_jaxpr/dot_general | solution.py:19
  15.0 0.4 fusion.28
  15.4 4.6 %fusion.30 = f32[512,128]{1,0:T(8,128)S(1)} fusion(f32[1024,512]{1,0:T(8,128)S(1)} %get-tuple-element.230, f32[512]{0:T(512)S(1)} %select_maximum_fusion.5, f32[8192,128]{1,0:T(8,128)} %get-tuple-element.261, s32[]{:T(128)S(6)} %select_n.27, f32[512,128]{1,0:T(8,128)S(1)} %get-tuple-element.247, f32[512]{0:T(512)S(1)} %get-tuple-element.232, ...), kind=kOutput, calls=%fused_computation.5.clone.1 | convolution fusion | flops 806551552 | bytes 3149829 | tf_op jit(solution)/shard_map/while/body/eval_jaxpr/dot_general | solution.py:19
  20.0 2.9 %multiply_reduce_fusion.2 = (f32[512]{0:T(512)S(1)}, f32[1024,512]{1,0:T(8,128)S(1)}) fusion(f32[512,128]{1,0:T(8,128)S(1)} %get-tuple-element.260, f32[8192,128]{1,0:T(8,128)} %get-tuple-element.259, s32[]{:T(128)S(6)} %select_n.27), kind=kOutput, calls=%fused_computation.2.clone.1 | convolution fusion | flops 806354432 | bytes 2885636 | tf_op jit(solution)/shard_map/while/body/eval_jaxpr/dot_general | solution.py:19
  23.0 0.4 fusion.28
  23.4 4.6 %fusion.30 = f32[512,128]{1,0:T(8,128)S(1)} fusion(f32[1024,512]{1,0:T(8,128)S(1)} %get-tuple-element.230, f32[512]{0:T(512)S(1)} %select_maximum_fusion.5, f32[8192,128]{1,0:T(8,128)} %get-tuple-element.261, s32[]{:T(128)S(6)} %select_n.27, f32[512,128]{1,0:T(8,128)S(1)} %get-tuple-element.247, f32[512]{0:T(512)S(1)} %get-tuple-element.232, ...), kind=kOutput, calls=%fused_computation.5.clone.1 | convolution fusion | flops 806551552 | bytes 3149829 | tf_op jit(solution)/shard_map/while/body/eval_jaxpr/dot_general | solution.py:19
  28.1 2.9 %multiply_reduce_fusion.2 = (f32[512]{0:T(512)S(1)}, f32[1024,512]{1,0:T(8,128)S(1)}) fusion(f32[512,128]{1,0:T(8,128)S(1)} %get-tuple-element.260, f32[8192,128]{1,0:T(8,128)} %get-tuple-element.259, s32[]{:T(128)S(6)} %select_n.27), kind=kOutput, calls=%fused_computation.2.clone.1 | convolution fusion | flops 806354432 | bytes 2885636 | tf_op jit(solution)/shard_map/while/body/eval_jaxpr/dot_general | solution.py:19
  31.0 0.4 fusion.28
  31.4 4.6 %fusion.30 = f32[512,128]{1,0:T(8,128)S(1)} fusion(f32[1024,512]{1,0:T(8,128)S(1)} %get-tuple-element.230, f32[512]{0:T(512)S(1)} %select_maximum_fusion.5, f32[8192,128]{1,0:T(8,128)} %get-tuple-element.261, s32[]{:T(128)S(6)} %select_n.27, f32[512,128]{1,0:T(8,128)S(1)} %get-tuple-element.247, f32[512]{0:T(512)S(1)} %get-tuple-element.232, ...), kind=kOutput, calls=%fused_computation.5.clone.1 | convolution fusion | flops 806551552 | bytes 3149829 | tf_op jit(solution)/shard_map/while/body/eval_jaxpr/dot_general | solution.py:19
  36.1 2.9 %multiply_reduce_fusion.2 = (f32[512]{0:T(512)S(1)}, f32[1024,512]{1,0:T(8,128)S(1)}) fusion(f32[512,128]{1,0:T(8,128)S(1)} %get-tuple-element.260, f32[8192,128]{1,0:T(8,128)} %get-tuple-element.259, s32[]{:T(128)S(6)} %select_n.27), kind=kOutput, calls=%fused_computation.2.clone.1 | convolution fusion | flops 806354432 | bytes 2885636 | tf_op jit(solution)/shard_map/while/body/eval_jaxpr/dot_general | solution.py:19
  39.0 0.4 fusion.28
  39.4 4.6 %fusion.30 = f32[512,128]{1,0:T(8,128)S(1)} fusion(f32[1024,512]{1,0:T(8,128)S(1)} %get-tuple-element.230, f32[512]{0:T(512)S(1)} %select_maximum_fusion.5, f32[8192,128]{1,0:T(8,128)} %get-tuple-element.261, s32[]{:T(128)S(6)} %select_n.27, f32[512,128]{1,0:T(8,128)S(1)} %get-tuple-element.247, f32[512]{0:T(512)S(1)} %get-tuple-element.232, ...), kind=kOutput, calls=%fused_computation.5.clone.1 | convolution fusion | flops 806551552 | bytes 3149829 | tf_op jit(solution)/shard_map/while/body/eval_jaxpr/dot_general | solution.py:19
  44.1 2.9 %multiply_reduce_fusion.2 = (f32[512]{0:T(512)S(1)}, f32[1024,512]{1,0:T(8,128)S(1)}) fusion(f32[512,128]{1,0:T(8,128)S(1)} %get-tuple-element.260, f32[8192,128]{1,0:T(8,128)} %get-tuple-element.259, s32[]{:T(128)S(6)} %select_n.27), kind=kOutput, calls=%fused_computation.2.clone.1 | convolution fusion | flops 806354432 | bytes 2885636 | tf_op jit(solution)/shard_map/while/body/eval_jaxpr/dot_general | solution.py:19
  47.0 0.4 fusion.28
  47.5 4.6 %fusion.30 = f32[512,128]{1,0:T(8,128)S(1)} fusion(f32[1024,512]{1,0:T(8,128)S(1)} %get-tuple-element.230, f32[512]{0:T(512)S(1)} %select_maximum_fusion.5, f32[8192,128]{1,0:T(8,128)} %get-tuple-element.261, s32[]{:T(128)S(6)} %select_n.27, f32[512,128]{1,0:T(8,128)S(1)} %get-tuple-element.247, f32[512]{0:T(512)S(1)} %get-tuple-element.232, ...), kind=kOutput, calls=%fused_computation.5.clone.1 | convolution fusion | flops 806551552 | bytes 3149829 | tf_op jit(solution)/shard_map/while/body/eval_jaxpr/dot_general | solution.py:19
  52.1 2.9 %multiply_reduce_fusion.2 = (f32[512]{0:T(512)S(1)}, f32[1024,512]{1,0:T(8,128)S(1)}) fusion(f32[512,128]{1,0:T(8,128)S(1)} %get-tuple-element.260, f32[8192,128]{1,0:T(8,128)} %get-tuple-element.259, s32[]{:T(128)S(6)} %select_n.27), kind=kOutput, calls=%fused_computation.2.clone.1 | convolution fusion | flops 806354432 | bytes 2885636 | tf_op jit(solution)/shard_map/while/body/eval_jaxpr/dot_general | solution.py:19
  55.0 0.4 fusion.28
  55.5 4.6 %fusion.30 = f32[512,128]{1,0:T(8,128)S(1)} fusion(f32[1024,512]{1,0:T(8,128)S(1)} %get-tuple-element.230, f32[512]{0:T(512)S(1)} %select_maximum_fusion.5, f32[8192,128]{1,0:T(8,128)} %get-tuple-element.261, s32[]{:T(128)S(6)} %select_n.27, f32[512,128]{1,0:T(8,128)S(1)} %get-tuple-element.247, f32[512]{0:T(512)S(1)} %get-tuple-element.232, ...), kind=kOutput, calls=%fused_computation.5.clone.1 | convolution fusion | flops 806551552 | bytes 3149829 | tf_op jit(solution)/shard_map/while/body/eval_jaxpr/dot_general | solution.py:19
  60.1 2.9 %multiply_reduce_fusion.2 = (f32[512]{0:T(512)S(1)}, f32[1024,512]{1,0:T(8,128)S(1)}) fusion(f32[512,128]{1,0:T(8,128)S(1)} %get-tuple-element.260, f32[8192,128]{1,0:T(8,128)} %get-tuple-element.259, s32[]{:T(128)S(6)} %select_n.27), kind=kOutput, calls=%fused_computation.2.clone.1 | convolution fusion | flops 806354432 | bytes 2885636 | tf_op jit(solution)/shard_map/while/body/eval_jaxpr/dot_general | solution.py:19
  63.1 0.4 fusion.28
  63.5 4.6 %fusion.30 = f32[512,128]{1,0:T(8,128)S(1)} fusion(f32[1024,512]{1,0:T(8,128)S(1)} %get-tuple-element.230, f32[512]{0:T(512)S(1)} %select_maximum_fusion.5, f32[8192,128]{1,0:T(8,128)} %get-tuple-element.261, s32[]{:T(128)S(6)} %select_n.27, f32[512,128]{1,0:T(8,128)S(1)} %get-tuple-element.247, f32[512]{0:T(512)S(1)} %get-tuple-element.232, ...), kind=kOutput, calls=%fused_computation.5.clone.1 | convolution fusion | flops 806551552 | bytes 3149829 | tf_op jit(solution)/shard_map/while/body/eval_jaxpr/dot_general | solution.py:19
  68.3 0.1 copy.7
  68.5 1.2 fusion.18
  69.6 0.3 fusion.12
  70.0 0.2 copy.8
  70.2 89.5 %shard_map.46 = f32[512,128]{1,0:T(8,128)S(1)} custom-call(f32[8,64,256]{2,1,0:T(8,128)S(1)} %bitcast.11, f32[512,512]{1,0:T(8,128)S(1)} %get-tuple-element.178.kept_ref), custom_call_target="tpu_custom_call" | custom-call | tf_op jit(solution)/shard_map/pallas_call | solution.py:229
  159.7 0.7 copy.23
  (30 shorter events, 0.3 us)
Async XLA Ops:
  0.0 4.0 %copy-start = (f32[512,128]{1,0:T(8,128)S(1)}, f32[512,128]{1,0:T(8,128)}, u32[]{:S(2)}) copy-start(f32[512,128]{1,0:T(8,128)} %param.6) | copy-start | bytes 786436

commit v3 on v2

--- a/solution.py
+++ b/solution.py
@@ -254,12 +254,81 @@
     )(part.reshape(ka_size, ka_share, 2 * width), kept_exponent)
 
 
+def thirds(value):
+    first = value.astype(jnp.bfloat16)
+    rest = value - first.astype(jnp.float32)
+    second = rest.astype(jnp.bfloat16)
+    third = (rest - second.astype(jnp.float32)).astype(jnp.bfloat16)
+    return first, second, third
+
+
+def target_kernel(inverse_root, queries_ref, keys_ref, values_ref, kept_ref, part_ref, wide, top, total, sums):
+    width = queries_ref.shape[1]
+
+    @pl.when(pl.program_id(0) == 0)
+    def _():
+        one, two, three = thirds(queries_ref[...])
+        wide[...] = jnp.concatenate((one, one, two, one, three, two), axis=1)
+        top[...] = jnp.full_like(top, -jnp.inf)
+        total[...] = jnp.zeros_like(total)
+        sums[...] = jnp.zeros_like(sums)
+
+    one, two, three = thirds(keys_ref[...])
+    scores = (
+        lax.dot_general(
+            wide[...],
+            jnp.concatenate((one, two, one, three, one, two), axis=1),
+            (((1,), (1,)), ((), ())),
+            preferred_element_type=jnp.float32,
+        )
+        * inverse_root
+    )
+    top_next = jnp.maximum(top[...], jnp.max(scores, axis=1, keepdims=True))
+    factor = jnp.exp(top[...] - top_next)
+    exponent = jnp.exp(scores - top_next)
+    top[...] = top_next
+    total[...] = total[...] * factor + jnp.sum(exponent, axis=1, keepdims=True)
+    one, two, three = thirds(values_ref[...])
+    high, middle, low = thirds(exponent)
+    pair = jnp.concatenate((one, two), axis=1)
+    product = functools.partial(jnp.dot, preferred_element_type=jnp.float32)
+    both = product(high, pair) + product(middle, pair)
+    small = product(high, three) + product(low, one)
+    sums[...] = sums[...] * factor + (both[:, :width] + (both[:, width:] + small))
+
+    @pl.when(pl.program_id(0) == pl.num_programs(0) - 1)
+    def _():
+        lane = lax.broadcasted_iota(jnp.int32, kept_ref.shape, 1)
+        stats = jnp.where(lane == 0, top[...], jnp.where(lane == 1, total[...], kept_ref[...]))
+        part_ref[:, :width] = sums[...]
+        part_ref[:, width:] = stats
+
+
+def target_part(queries, cache_keys, cache_values, kept_stats, inverse_root):
+    query_rows, width = queries.shape
+    block_size = min(1024, cache_keys.shape[0])
+    fixed = pl.BlockSpec((query_rows, width), lambda block: (0, 0))
+    moving = pl.BlockSpec((block_size, width), lambda block: (block, 0))
+    return pl.pallas_call(
+        functools.partial(target_kernel, inverse_root),
+        grid=(cache_keys.shape[0] // block_size,),
+        out_shape=jax.ShapeDtypeStruct((query_rows, 2 * width), jnp.float32),
+        in_specs=[fixed, moving, moving, fixed],
+        out_specs=pl.BlockSpec((query_rows, 2 * width), lambda block: (0, 0)),
+        scratch_shapes=[
+            pltpu.VMEM((query_rows, 6 * width), jnp.bfloat16),
+            pltpu.VMEM((query_rows, 1), jnp.float32),
+            pltpu.VMEM((query_rows, 1), jnp.float32),
+            pltpu.VMEM((query_rows, width), jnp.float32),
+        ],
+        compiler_params=pltpu.CompilerParams(vmem_limit_bytes=40 * 1024 * 1024),
+    )(queries, cache_keys, cache_values, kept_stats)
+
+
 def shards(queries, cache_keys, cache_values, kept_index):
-    query_rows, head_width = queries.shape
+    head_width = queries.shape[1]
     inverse_root = 1.0 / math.sqrt(head_width)
     cache_rows = cache_keys.shape[0]
-    block_size = min(1024, cache_rows)
-    blocks = cache_rows // block_size
 
     local_kept = kept_index - lax.axis_index("ka") * cache_rows
     kept_keys = jnp.take(cache_keys, local_kept, axis=0)
@@ -268,35 +337,12 @@
     kept_exponent = jnp.exp(kept_scores - kept_top[:, None])
     kept_total = jnp.sum(kept_exponent, axis=1)
 
-    def step(block_number, state):
-        top, total, numerator = state
-        start = block_number * block_size
-        keys_block = lax.dynamic_slice_in_dim(cache_keys, start, block_size, axis=0)
-        values_block = lax.dynamic_slice_in_dim(cache_values, start, block_size, axis=0)
-        scores = contract(queries, keys_block, 1, 1) * inverse_root
-        top_next = jnp.maximum(top, jnp.max(scores, axis=1))
-        factor = jnp.exp(top - top_next)
-        exponent = jnp.exp(scores - top_next[:, None])
-        return (
-            top_next,
-            total * factor + jnp.sum(exponent, axis=1),
-            numerator * factor[:, None] + contract(exponent, values_block, 1, 0),
-        )
-
-    top, total, numerator = lax.fori_loop(
-        0,
-        blocks,
-        step,
-        (
-            jnp.full((query_rows,), -jnp.inf, jnp.float32),
-            jnp.zeros((query_rows,), jnp.float32),
-            jnp.zeros((query_rows, head_width), jnp.float32),
-        ),
+    zero = jnp.zeros_like(kept_top)
+    stats = jnp.stack((zero, zero, kept_top, kept_total), axis=1)
+    stats = jnp.pad(stats, ((0, 0), (0, head_width - 4)))
+    return fit(
+        target_part(queries, cache_keys, cache_values, stats, inverse_root), kept_exponent
     )
-
-    stats = jnp.stack((top, total, kept_top, kept_total), axis=1)
-    stats = jnp.pad(stats, ((0, 0), (0, head_width - 4)))
-    return fit(jnp.concatenate((numerator, stats), axis=1), kept_exponent)
 
 
 def solution(mesh):

time: 161 us -> 125 us (0.78)
  matrix products: 61.5 us -> 2.13 us
  Pallas kernels: 89.5 us -> 113 us
  local copies, waits for them, and re-layouts: 4.27 us -> 8.48 us
  other arithmetic: 4.49 us -> 1.11 us
    dot_general x17 -> x1, matrix products: 61.5 us -> 2.13 us  [contract(): lax.dot_general(left_side, right_side, (((left_dim,), (right_dim,)), ((),...]
    pallas_call x0 -> x1, Pallas kernels: none -> 23.1 us  [target_part(): pl.pallas_call(functools.partial(target_kernel, inverse_root), grid=(cach...]
    unnamed x3 -> x7, local copies, waits for them, and re-layouts: 0.71 us -> 5.08 us
    reduce_sum x8 -> x0, other arithmetic: 3.21 us -> none  [step(): jnp.sum(exponent, axis=1)]
where the time goes in v3:
time: 125 us; the launch traced here: 124 us
  Pallas kernels  113 us (90%)
  local copies, waits for them, and re-layouts  8.48 us (7%)
  matrix products  2.13 us (2%)
    pallas_call x1, Pallas kernels, fit(): pl.pallas_call(functools.partial(fit_kernel, ka_size, pb_size), out_shape...  89.5 us
    pallas_call x1, Pallas kernels, target_part(): pl.pallas_call(functools.partial(target_kernel, inverse_root), grid=(cach...  23.1 us
    unnamed x7, local copies, waits for them, and re-layouts  5.08 us
    gather x1, local copies, waits for them, and re-layouts, shards(): kept_keys = jnp.take(cache_keys, local_kept, axis=0)  3.22 us

profile of v3, /device:TPU:0, one launch (start us, length us, event | category | flops | bytes accessed | tf_op | source)
XLA Modules:
  0.0 124.4 jit_solution(18107318994761089747)
XLA Ops:
  0.0 0.0 copy-start.2
  0.0 0.7 compare_and_fusion
  0.7 3.2 %gather_fusion = f32[512,128]{1,0:T(8,128)S(1)} fusion(f32[8192,128]{1,0:T(8,128)} %keys_ref.1, s32[1024]{0:T(1024)S(1)} %pad_clamp_fusion), kind=kCustom, calls=%fused_computation | custom fusion | bytes 526336 | tf_op jit(solution)/shard_map/jit(_take)/gather | solution.py:334
  4.0 2.1 %fusion.6 = (f32[512]{0:T(512)S(1)}, f32[512,512]{0,1:T(8,128)S(1)}) fusion(f32[512,128]{1,0:T(8,128)} %queries_ref.1, f32[512,128]{1,0:T(8,128)S(1)} %gather_fusion, pred[512]{0:T(512)(128)(4,1)S(1)} %get-tuple-element.5), kind=kOutput, calls=%fused_computation.13 | convolution fusion | flops 403242496 | bytes 1575424 | tf_op jit(solution)/shard_map/dot_general | solution.py:19
  6.1 0.3 fusion
  6.4 0.1 pad_maximum_fusion
  6.5 0.1 copy.10
  6.7 0.0 copy-done.2
  6.7 0.0 copy-start
  6.7 2.2 %copy-done = f32[8192,128]{1,0:T(8,128)S(1)} copy-done((f32[8192,128]{1,0:T(8,128)S(1)}, f32[8192,128]{1,0:T(8,128)}, u32[]{:S(2)}) %copy-start) | copy-done | bytes 4194328
  8.9 0.0 copy-start.1
  8.9 2.2 %copy-done.1 = f32[8192,128]{1,0:T(8,128)S(1)} copy-done((f32[8192,128]{1,0:T(8,128)S(1)}, f32[8192,128]{1,0:T(8,128)}, u32[]{:S(2)}) %copy-start.1) | copy-done | bytes 4194328
  11.1 23.1 %shard_map.46 = f32[512,256]{1,0:T(8,128)S(1)} custom-call(f32[512,128]{1,0:T(8,128)S(1)} %copy-done.2, f32[8192,128]{1,0:T(8,128)S(1)} %copy-done, f32[8192,128]{1,0:T(8,128)S(1)} %copy-done.1, f32[512,128]{1,0:T(8,128)S(1)} %pad.4.kept_ref), custom_call_target="tpu_custom_call" | custom-call | tf_op jit(solution)/shard_map/pallas_call | solution.py:312
  34.2 89.5 %shard_map.47 = f32[512,128]{1,0:T(8,128)S(1)} custom-call(f32[8,64,256]{2,1,0:T(8,128)S(1)} %bitcast.6, f32[512,512]{1,0:T(8,128)S(1)} %get-tuple-element.7.kept_ref), custom_call_target="tpu_custom_call" | custom-call | tf_op jit(solution)/shard_map/pallas_call | solution.py:229
  123.6 0.7 copy.13
  (4 shorter events, 0.0 us)
Async XLA Ops:
  0.0 6.7 %copy-start.2 = (f32[512,128]{1,0:T(8,128)S(1)}, f32[512,128]{1,0:T(8,128)}, u32[]{:S(2)}) copy-start(f32[512,128]{1,0:T(8,128)} %queries_ref.1) | copy-start | bytes 786436
  6.7 2.2 %copy-start = (f32[8192,128]{1,0:T(8,128)S(1)}, f32[8192,128]{1,0:T(8,128)}, u32[]{:S(2)}) copy-start(f32[8192,128]{1,0:T(8,128)} %keys_ref.1) | copy-start | bytes 12582916
  8.9 2.2 %copy-start.1 = (f32[8192,128]{1,0:T(8,128)S(1)}, f32[8192,128]{1,0:T(8,128)}, u32[]{:S(2)}) copy-start(f32[8192,128]{1,0:T(8,128)} %values_ref.1) | copy-start | bytes 12582916

commit v4 on v3

--- a/solution.py
+++ b/solution.py
@@ -306,7 +306,7 @@
 
 def target_part(queries, cache_keys, cache_values, kept_stats, inverse_root):
     query_rows, width = queries.shape
-    block_size = min(1024, cache_keys.shape[0])
+    block_size = min(2048, cache_keys.shape[0])
     fixed = pl.BlockSpec((query_rows, width), lambda block: (0, 0))
     moving = pl.BlockSpec((block_size, width), lambda block: (block, 0))
     return pl.pallas_call(

time: 125 us -> 123 us (0.984)
  Pallas kernels: 113 us -> 111 us
    pallas_call x1, Pallas kernels: 23.1 us -> 21 us  [target_part(): pl.pallas_call(functools.partial(target_kernel, inverse_root), grid=(cach...]
where the time goes in v4:
time: 123 us; the launch traced here: 122 us
  Pallas kernels  111 us (90%)
  local copies, waits for them, and re-layouts  8.47 us (7%)
  matrix products  2.13 us (2%)
    pallas_call x1, Pallas kernels, fit(): pl.pallas_call(functools.partial(fit_kernel, ka_size, pb_size), out_shape...  89.6 us
    pallas_call x1, Pallas kernels, target_part(): pl.pallas_call(functools.partial(target_kernel, inverse_root), grid=(cach...  21 us
    unnamed x7, local copies, waits for them, and re-layouts  5.08 us
    gather x1, local copies, waits for them, and re-layouts, shards(): kept_keys = jnp.take(cache_keys, local_kept, axis=0)  3.22 us

profile of v4, /device:TPU:0, one launch (start us, length us, event | category | flops | bytes accessed | tf_op | source)
XLA Modules:
  0.0 122.3 jit_solution(1732357622051276504)
XLA Ops:
  0.0 0.0 copy-start.2
  0.0 0.7 compare_and_fusion
  0.7 3.2 %gather_fusion = f32[512,128]{1,0:T(8,128)S(1)} fusion(f32[8192,128]{1,0:T(8,128)} %keys_ref.1, s32[1024]{0:T(1024)S(1)} %pad_clamp_fusion), kind=kCustom, calls=%fused_computation | custom fusion | bytes 526336 | tf_op jit(solution)/shard_map/jit(_take)/gather | solution.py:334
  4.0 2.1 %fusion.6 = (f32[512]{0:T(512)S(1)}, f32[512,512]{0,1:T(8,128)S(1)}) fusion(f32[512,128]{1,0:T(8,128)} %queries_ref.1, f32[512,128]{1,0:T(8,128)S(1)} %gather_fusion, pred[512]{0:T(512)(128)(4,1)S(1)} %get-tuple-element.5), kind=kOutput, calls=%fused_computation.13 | convolution fusion | flops 403242496 | bytes 1575424 | tf_op jit(solution)/shard_map/dot_general | solution.py:19
  6.1 0.3 fusion
  6.4 0.1 pad_maximum_fusion
  6.5 0.1 copy.10
  6.7 0.0 copy-done.2
  6.7 0.0 copy-start
  6.7 2.2 %copy-done = f32[8192,128]{1,0:T(8,128)S(1)} copy-done((f32[8192,128]{1,0:T(8,128)S(1)}, f32[8192,128]{1,0:T(8,128)}, u32[]{:S(2)}) %copy-start) | copy-done | bytes 4194328
  8.9 0.0 copy-start.1
  8.9 2.2 %copy-done.1 = f32[8192,128]{1,0:T(8,128)S(1)} copy-done((f32[8192,128]{1,0:T(8,128)S(1)}, f32[8192,128]{1,0:T(8,128)}, u32[]{:S(2)}) %copy-start.1) | copy-done | bytes 4194328
  11.1 21.0 %shard_map.46 = f32[512,256]{1,0:T(8,128)S(1)} custom-call(f32[512,128]{1,0:T(8,128)S(1)} %copy-done.2, f32[8192,128]{1,0:T(8,128)S(1)} %copy-done, f32[8192,128]{1,0:T(8,128)S(1)} %copy-done.1, f32[512,128]{1,0:T(8,128)S(1)} %pad.4.kept_ref), custom_call_target="tpu_custom_call" | custom-call | tf_op jit(solution)/shard_map/pallas_call | solution.py:312
  32.1 89.6 %shard_map.47 = f32[512,128]{1,0:T(8,128)S(1)} custom-call(f32[8,64,256]{2,1,0:T(8,128)S(1)} %bitcast.6, f32[512,512]{1,0:T(8,128)S(1)} %get-tuple-element.7.kept_ref), custom_call_target="tpu_custom_call" | custom-call | tf_op jit(solution)/shard_map/pallas_call | solution.py:229
  121.6 0.7 copy.13
  (4 shorter events, 0.0 us)
Async XLA Ops:
  0.0 6.7 %copy-start.2 = (f32[512,128]{1,0:T(8,128)S(1)}, f32[512,128]{1,0:T(8,128)}, u32[]{:S(2)}) copy-start(f32[512,128]{1,0:T(8,128)} %queries_ref.1) | copy-start | bytes 786436
  6.7 2.2 %copy-start = (f32[8192,128]{1,0:T(8,128)S(1)}, f32[8192,128]{1,0:T(8,128)}, u32[]{:S(2)}) copy-start(f32[8192,128]{1,0:T(8,128)} %keys_ref.1) | copy-start | bytes 12582916
  8.9 2.2 %copy-start.1 = (f32[8192,128]{1,0:T(8,128)S(1)}, f32[8192,128]{1,0:T(8,128)}, u32[]{:S(2)}) copy-start(f32[8192,128]{1,0:T(8,128)} %values_ref.1) | copy-start | bytes 12582916
